TPU v7x, 512 devices: a whole 4x8x8 slice. The times are simulated.
512 devices in a mesh: prow: 32 (over y, x), pcol: 16 (over z, core).
Axes of the slice: x: 4, y: 8, z: 8, core: 2. Of those that a mesh axis runs over, the one named last changes fastest.
Arguments:
- matrix: bfloat16 [4, 8192, 4, 4096], P(None, 'prow', None, 'pcol'), may hold values from -6 to 6
- pivots: int32 [2, 256], replicated, may hold values from 0 to 32767, as said below
- lower_inverse: bfloat16 [2, 256, 256], replicated, as said below
- upper_inverse: bfloat16 [2, 256, 256], replicated, as said below
Outputs:
- factored: bfloat16 [4, 8192, 4, 4096], P(None, 'prow', None, 'pcol')
Inputs may be any that keep to these rules, and one draw needn't show every extreme that they name: For each panel k and each i, pivots[k, i] is either k * 256 + i or a row at or after (k + 1) * 256; entry 0 of each list is k * 256; the rows of one panel's list are distinct, and each list names row 32767. Each lower_inverse[k] is unit lower triangular. Each upper_inverse[k] is upper triangular with positive diagonal.
All inputs are finite; a program needn't handle non-finite values.
Results may differ from a plain program's by a relative error of at most 0.0079.
Values may be sent and summed in bfloat16 or wider, within the bound.
A program may use at most 64 MiB of HBM per device.

v0:
```python
import jax
import jax.numpy as jnp
from jax import lax
from jax.sharding import PartitionSpec as P


def spread(block, axis, source):
    block = jnp.where(lax.axis_index(axis) == source, block, jnp.zeros_like(block))
    return lax.psum(block, axis)


def local(matrix, pivots, lower_inverse, upper_inverse):
    row_count = lax.axis_size("prow")
    col_count = lax.axis_size("pcol")
    my_row = lax.axis_index("prow")
    my_col = lax.axis_index("pcol")
    blocks_down, block, blocks_across, _ = matrix.shape
    local_rows = blocks_down * block
    local_cols = blocks_across * block
    current = matrix.reshape(local_rows, local_cols)
    row_place = jnp.arange(local_rows)
    col_place = jnp.arange(local_cols)
    global_rows = (row_place // block * row_count + my_row) * block + row_place % block
    global_cols = (col_place // block * col_count + my_col) * block + col_place % block
    for panel in range(pivots.shape[0]):
        start = panel * block
        chosen = pivots[panel]
        block_row = chosen // block
        is_mine = block_row % row_count == my_row
        local_index = block_row // row_count * block + chosen % block
        safe_index = jnp.where(is_mine, local_index, 0)
        picked = jnp.where(is_mine[:, None], current[safe_index], jnp.zeros((), jnp.bfloat16))
        top_holder = panel % row_count
        top_first = panel // row_count * block
        is_top = my_row == top_holder
        top_local = current[top_first : top_first + block]
        incoming = lax.psum(picked, "prow").astype(jnp.float32)
        old_top = spread(top_local, "prow", top_holder)
        incoming = incoming.astype(jnp.bfloat16)
        target = jnp.where(is_mine, local_index, local_rows)
        current = current.at[target].set(old_top, mode="drop")
        top_now = current[top_first : top_first + block]
        current = current.at[top_first : top_first + block].set(
            jnp.where(is_top, incoming, top_now)
        )
        panel_holder = panel % col_count
        panel_first = panel // col_count * block
        panel_cols = current[:, panel_first : panel_first + block]
        factor = jnp.dot(
            panel_cols, upper_inverse[panel], preferred_element_type=jnp.float32
        ).astype(jnp.bfloat16)
        lower = spread(factor, "pcol", panel_holder)
        upper = jnp.dot(lower_inverse[panel], incoming, preferred_element_type=jnp.float32).astype(
            jnp.bfloat16
        )
        row_mask = global_rows >= start + block
        col_mask = global_cols >= start + block
        product = jnp.dot(lower, upper, preferred_element_type=jnp.float32)
        changed = (current.astype(jnp.float32) - product).astype(jnp.bfloat16)
        current = jnp.where(row_mask[:, None] & col_mask[None, :], changed, current)
        panel_now = current[:, panel_first : panel_first + block]
        is_panel = my_col == panel_holder
        current = current.at[:, panel_first : panel_first + block].set(
            jnp.where(is_panel & row_mask[:, None], lower, panel_now)
        )
        top_now = current[top_first : top_first + block]
        current = current.at[top_first : top_first + block].set(
            jnp.where(is_top & col_mask[None, :], upper, top_now)
        )
    return current.reshape(matrix.shape)


def solution(mesh):
    in_specs = (P(None, "prow", None, "pcol"), P(), P(), P())
    out_specs = P(None, "prow", None, "pcol")
    return jax.shard_map(local, mesh=mesh, in_specs=in_specs, out_specs=out_specs, check_vma=False)
```

profile of v0, /device:TPU:1, one launch (start us, length us, event | category | flops | bytes accessed | tf_op | source)
XLA Modules:
  0.0 609.7 jit_solution(5548198204034712789)
XLA Ops:
  6.5 0.8 and_select_fusion.5
  7.3 0.8 fusion.45
  8.1 2.1 copy.11
  10.2 1.3 slice_select_fusion.4
  11.5 0.9 copy.12
  12.4 1.2 gather_fusion
  13.5 0.9 broadcast_select_fusion.1
  14.6 161.5 %all-reduce.13.cloned.1.call-done = (bf16[256,1024]{1,0:T(8,128)(2,1)}, bf16[256,1024]{1,0:T(8,128)(2,1)}) async-done(((bf16[256,1024]{1,0:T(8,128)(2,1)}, bf16[256,1024]{1,0:T(8,128)(2,1)}), (bf16[256,1024]{1,0:T(8,128)(2,1)}, bf16[256,1024]{1,0:T(8,128)(2,1)})) %all-reduce.13.cloned.1.call-update) | async-done | bytes 1048592 | tf_op jit(solution)/shard_map/psum | solution.py:9
  176.1 3.3 scatter_fusion
  179.7 1.1 fusion
  181.9 116.9 %all-reduce.7.cloned.1.call-done = bf16[1024,256]{1,0:T(8,128)(2,1)} async-done(((bf16[1024,256]{1,0:T(8,128)(2,1)}), bf16[1024,256]{1,0:T(8,128)(2,1)}) %all-reduce.7.cloned.1.call-update) | async-done | bytes 524304 | tf_op jit(solution)/shard_map/psum | solution.py:9
  298.9 3.4 and_select_fusion
  302.2 2.9 fusion.2
  305.2 2.3 broadcast_select_fusion.2
  307.5 3.4 gather_fusion.1
  310.9 0.9 broadcast_select_fusion
  311.9 155.8 %all-reduce.11.cloned.1.call-done = (bf16[256,1024]{1,0:T(8,128)(2,1)}, bf16[256,1024]{1,0:T(8,128)(2,1)}) async-done(((bf16[256,1024]{1,0:T(8,128)(2,1)}, bf16[256,1024]{1,0:T(8,128)(2,1)}), (bf16[256,1024]{1,0:T(8,128)(2,1)}, bf16[256,1024]{1,0:T(8,128)(2,1)})) %all-reduce.11.cloned.1.call-update) | async-done | bytes 1048592 | tf_op jit(solution)/shard_map/psum | solution.py:9
  467.7 5.4 scatter_fusion.1
  473.1 2.0 fusion.6
  475.1 2.1 fusion.1
  477.6 117.9 %all-reduce.9.cloned.1.call-done = bf16[1024,256]{1,0:T(8,128)(2,1)} async-done(((bf16[1024,256]{1,0:T(8,128)(2,1)}), bf16[1024,256]{1,0:T(8,128)(2,1)}) %all-reduce.9.cloned.1.call-update) | async-done | bytes 524304 | tf_op jit(solution)/shard_map/psum | solution.py:9
  595.5 3.5 and_select_fusion.1
  599.1 1.1 fusion.3
  600.4 2.8 reshape.658
  (40 shorter events, 2.1 us)
Async XLA Ops:
  6.5 169.6 %all-reduce.13.cloned.1.call-start = ((), (), s32[]{:S(2)}) async-start(), calls=%async_computation.3 | async-start | bytes 2097152 | tf_op jit(solution)/shard_map/psum | solution.py:9
  14.5 284.4 %all-reduce.7.cloned.1.call-start = ((), (), s32[]{:S(2)}) async-start(), calls=%async_computation | async-start | bytes 1048576 | tf_op jit(solution)/shard_map/psum | solution.py:9
  176.1 3.4 copy-start
  176.1 3.6 copy-start.5
  179.5 2.2 copy-start.4
  180.8 286.9 %all-reduce.11.cloned.1.call-start = ((), (), s32[]{:S(2)}) async-start(), calls=%async_computation.2 | async-start | bytes 2097152 | tf_op jit(solution)/shard_map/psum | solution.py:9
  298.9 3.4 copy-start.2
  311.8 283.7 %all-reduce.9.cloned.1.call-start = ((), (), s32[]{:S(2)}) async-start(), calls=%async_computation.1 | async-start | bytes 1048576 | tf_op jit(solution)/shard_map/psum | solution.py:9
  467.7 5.4 copy-start.1
  467.7 7.4 %copy-start.6 = (bf16[2,256,256]{2,1,0:T(8,128)(2,1)S(1)}, bf16[2,256,256]{2,1,0:T(8,128)(2,1)}, u32[]{:S(2)}) copy-start(bf16[2,256,256]{2,1,0:T(8,128)(2,1)} %param.19) | copy-start | bytes 786436
  595.5 3.5 copy-start.3
Sparse Core Ops, SparseCore 0:
  14.6 161.4 all-reduce.12
  181.0 117.8 all-reduce.6
  311.9 155.7 all-reduce.10
  477.4 118.0 all-reduce.8
where the time goes:
time: 610 us
  waiting for transfers between devices  552 us (90%)
  local copies, waits for them, and re-layouts  19.8 us (3%)
  other arithmetic  13.5 us (2%)
  between operations  13.3 us (2%)
  matrix products  10.8 us (2%)
    psum x4, waiting for transfers between devices, spread(): return lax.psum(block, axis)  552 us
  transfers between devices with their start and end apart: 4, of which 4 were waited for; matrix products, arithmetic and copies ran while one was open for 0% of the time, Pallas kernels for 0%

commit v1 on v0

--- a/solution.py
+++ b/solution.py
@@ -6,7 +6,12 @@
 
 def spread(block, axis, source):
     block = jnp.where(lax.axis_index(axis) == source, block, jnp.zeros_like(block))
-    return lax.psum(block, axis)
+
+    def floor_unite(t0, shard_axis):
+        u_next = jax.lax.all_gather(t0, shard_axis).sum(axis=0)
+        return u_next
+
+    return floor_unite(block, axis)
 
 
 def local(matrix, pivots, lower_inverse, upper_inverse):

time: 610 us -> 797 us (1.31)
  waiting for transfers between devices: 552 us -> 687 us
  other arithmetic: 13.5 us -> 44.6 us
  local copies, waits for them, and re-layouts: 19.8 us -> 37.1 us
    all_gather x0 -> x4, waiting for transfers between devices: none -> 414 us  [floor_unite(): u_next = jax.lax.all_gather(t0, shard_axis).sum(axis=0)]
    psum x4 -> x2, waiting for transfers between devices: 552 us -> 273 us  [local(): incoming = lax.psum(picked, 'prow').astype(jnp.float32)]
    reduce_sum x0 -> x4, other arithmetic: none -> 27.1 us  [floor_unite(): u_next = jax.lax.all_gather(t0, shard_axis).sum(axis=0)]
    unnamed x16 -> x22, local copies, waits for them, and re-layouts: 3 us -> 12.4 us
  transfers between devices with their start and end apart: 4 -> 6, of which waited for: 4 -> 6; matrix products, arithmetic and copies ran while one was open for 0% -> 6% of each run, Pallas kernels for 0% -> 0%
where the time goes in v1:
time: 797 us
  waiting for transfers between devices  687 us (86%)
  other arithmetic  44.6 us (6%)
  local copies, waits for them, and re-layouts  37.1 us (5%)
  between operations  13.8 us (2%)
  matrix products  13.6 us (2%)
    all_gather x4, waiting for transfers between devices, floor_unite(): u_next = jax.lax.all_gather(t0, shard_axis).sum(axis=0)  414 us
    psum x2, waiting for transfers between devices, local(): incoming = lax.psum(picked, 'prow').astype(jnp.float32)  273 us
    reduce_sum x4, other arithmetic, floor_unite(): u_next = jax.lax.all_gather(t0, shard_axis).sum(axis=0)  27.1 us
  transfers between devices with their start and end apart: 6, of which 6 were waited for; matrix products, arithmetic and copies ran while one was open for 6% of the time, Pallas kernels for 0%

profile of v1, /device:TPU:1, one launch (start us, length us, event | category | flops | bytes accessed | tf_op | source)
XLA Modules:
  0.0 796.7 jit_solution(893697331869985858)
XLA Ops:
  13.5 147.8 %all-gather.8.cloned.1.call-done = bf16[32,256,1024]{2,1,0:T(8,128)(2,1)} async-done(((bf16[1,256,1024]{2,1,0:T(8,128)(2,1)}), bf16[32,256,1024]{2,1,0:T(8,128)(2,1)}) %all-gather.8.cloned.1.call-update) | async-done | bytes 16777232 | tf_op jit(solution)/shard_map/all_gather | solution.py:11
  161.3 9.1 %reduce_sum.48 = bf16[256,1024]{1,0:T(8,128)(2,1)S(1)} reduce(bf16[32,256,1024]{2,1,0:T(8,128)(2,1)} %all-gather.8.cloned.1.call-done, bf16[]{:T(256)} %constant.277.clone.1), dimensions={0}, to_apply=%region_0.1 | reduce | flops 8126464 | bytes 17301506 | tf_op jit(solution)/shard_map/reduce_sum | solution.py:11
  170.4 2.8 scatter_fusion
  173.3 2.6 copy.26
  175.8 140.6 %all-reduce.3.cloned.1.call-done = bf16[256,1024]{0,1:T(8,128)(2,1)} async-done(((bf16[256,1024]{0,1:T(8,128)(2,1)}), bf16[256,1024]{0,1:T(8,128)(2,1)}) %all-reduce.3.cloned.1.call-update) | async-done | bytes 524304 | tf_op jit(solution)/shard_map/psum | solution.py:42
  318.6 2.2 fusion
  322.7 59.7 %all-gather.10.cloned.1.call-done = bf16[16384,256]{1,0:T(8,128)(2,1)} async-done(((bf16[1024,256]{1,0:T(8,128)(2,1)}), bf16[16384,256]{1,0:T(8,128)(2,1)}) %all-gather.10.cloned.1.call-update) | async-done | bytes 8388624 | tf_op jit(solution)/shard_map/all_gather | solution.py:11
  382.4 5.0 reduce_sum.49
  387.7 3.4 and_select_fusion
  391.1 2.6 fusion.2
  393.6 2.3 broadcast_select_fusion.1
  396.1 2.9 copy.29
  401.5 145.6 %all-gather.12.cloned.1.call-done = bf16[8192,1024]{0,1:T(8,128)(2,1)} async-done(((bf16[256,1024]{0,1:T(8,128)(2,1)}), bf16[8192,1024]{0,1:T(8,128)(2,1)}) %all-gather.12.cloned.1.call-update) | async-done | bytes 16777232 | tf_op jit(solution)/shard_map/all_gather | solution.py:11
  547.1 10.3 %copy.41 = bf16[128,8,32,256]{3,2,1,0:T(8,128)(2,1)S(1)} copy(bf16[128,8,32,256]{3,1,2,0:T(8,128)(2,1)} %bitcast.70) | data formatting | bytes 33554432
  557.4 8.1 %bitcast_reduce_fusion = bf16[256,1024]{0,1:T(8,128)(2,1)S(1)} fusion(bf16[128,8,32,256]{3,2,1,0:T(8,128)(2,1)S(1)} %copy.41), kind=kLoop, calls=%fused_computation.4 | loop fusion | flops 8126464 | bytes 17301504 | tf_op jit(solution)/shard_map/reduce_sum | solution.py:11
  565.7 2.8 scatter_fusion.1
  568.6 2.6 copy.34
  571.1 132.9 %all-reduce.5.cloned.1.call-done = bf16[256,1024]{0,1:T(8,128)(2,1)} async-done(((bf16[256,1024]{0,1:T(8,128)(2,1)}), bf16[256,1024]{0,1:T(8,128)(2,1)}) %all-reduce.5.cloned.1.call-update) | async-done | bytes 524304 | tf_op jit(solution)/shard_map/psum | solution.py:42
  709.6 60.5 %all-gather.14.cloned.1.call-done = bf16[16384,256]{1,0:T(8,128)(2,1)} async-done(((bf16[1024,256]{1,0:T(8,128)(2,1)}), bf16[16384,256]{1,0:T(8,128)(2,1)}) %all-gather.14.cloned.1.call-update) | async-done | bytes 8388624 | tf_op jit(solution)/shard_map/all_gather | solution.py:11
  770.1 5.0 reduce_sum.51
  775.3 3.4 and_select_fusion.1
  778.7 2.6 fusion.3
  783.3 3.3 reshape.668
  786.6 3.2 copy.37
  (68 shorter events, 21.7 us)
Async XLA Ops:
  6.5 154.8 %all-gather.8.cloned.1.call-start = ((), (), s32[]{:S(2)}) async-start(), calls=%async_computation | async-start | bytes 17301504 | tf_op jit(solution)/shard_map/all_gather | solution.py:11
  9.0 307.4 %all-reduce.3.cloned.1.call-start = ((), (), s32[]{:S(2)}) async-start(), calls=%async_computation.1 | async-start | bytes 1048576 | tf_op jit(solution)/shard_map/psum | solution.py:42
  9.0 2.1 copy-start.7
  13.5 369.0 %all-gather.10.cloned.1.call-start = ((), (), s32[]{:S(2)}) async-start(), calls=%async_computation.3 | async-start | bytes 8912896 | tf_op jit(solution)/shard_map/all_gather | solution.py:11
  173.3 145.3 %copy-start.8 = (bf16[2,256,256]{2,1,0:T(8,128)(2,1)S(1)}, bf16[2,256,256]{2,1,0:T(8,128)(2,1)}, u32[]{:S(2)}) copy-start(bf16[2,256,256]{2,1,0:T(8,128)(2,1)} %param.19) | copy-start | bytes 786436
  175.8 145.7 %copy-start.6 = (bf16[2,256,256]{2,1,0:T(8,128)(2,1)S(1)}, bf16[2,256,256]{2,1,0:T(8,128)(2,1)}, u32[]{:S(2)}) copy-start(bf16[2,256,256]{2,1,0:T(8,128)(2,1)} %param.18) | copy-start | bytes 786436
  316.4 5.2 copy-start.2
  320.9 226.3 %all-gather.12.cloned.1.call-start = ((), (), s32[]{:S(2)}) async-start(), calls=%async_computation.4 | async-start | bytes 17301504 | tf_op jit(solution)/shard_map/all_gather | solution.py:11
  382.4 5.2 copy-start
  387.6 6.0 copy-start.4
  396.0 308.1 %all-reduce.5.cloned.1.call-start = ((), (), s32[]{:S(2)}) async-start(), calls=%async_computation.2 | async-start | bytes 1048576 | tf_op jit(solution)/shard_map/psum | solution.py:42
  401.2 368.8 %all-gather.14.cloned.1.call-start = ((), (), s32[]{:S(2)}) async-start(), calls=%async_computation.5 | async-start | bytes 8912896 | tf_op jit(solution)/shard_map/all_gather | solution.py:11
  568.6 137.5 %copy-start.9 = (bf16[2,256,256]{2,1,0:T(8,128)(2,1)S(1)}, bf16[2,256,256]{2,1,0:T(8,128)(2,1)}, u32[]{:S(2)}) copy-start(bf16[2,256,256]{2,1,0:T(8,128)(2,1)} %param.19) | copy-start | bytes 786436
  704.0 4.4 copy-start.3
  770.1 5.2 copy-start.1
  775.3 6.0 copy-start.5
Sparse Core Ops, SparseCore 0:
  10.5 150.7 all-gather.7
  164.7 151.6 all-reduce.2
  321.0 61.4 all-gather.9
  396.1 150.9 all-gather.11
  550.7 153.2 all-reduce.4
  708.4 61.5 all-gather.13
